TPU v7x, 128 devices: a whole 4x4x4 slice. The times are simulated.
128 devices in a mesh: fsdp: 4 (over y), ctx: 16 (over z, x), tp: 2 (over core).
Axes of the slice: x: 4, y: 4, z: 4, core: 2. Of those that a mesh axis runs over, the one named last changes fastest.
Arguments:
- inputs: float32 [8, 2048, 896], P('fsdp', 'ctx'), may hold values from -6 to 6
- block_order: int32 [8, 32], P('fsdp'), may hold values from 0 to 31, as said below
- cotangent: float32 [8, 2048, 896], P('fsdp', 'ctx'), may hold values from -6 to 6
- gains: bfloat16 [1, 2, 896], P(None, None, ('fsdp', 'ctx')), may hold values from 0.5 to 1.5
- w_qkv: bfloat16 [1, 896, 2, 576], P(None, ('fsdp', 'ctx'), 'tp'), may hold values from -0.1875 to 0.1875
- b_qkv: bfloat16 [1, 2, 9, 64], P(None, 'tp', None, ('fsdp', 'ctx')), may hold values from -1 to 1
- w_out: bfloat16 [1, 2, 448, 896], P(None, 'tp', None, ('fsdp', 'ctx')), may hold values from -1.5 to 1.5
- w_gate_up: bfloat16 [1, 896, 2, 4864], P(None, ('fsdp', 'ctx'), None, 'tp'), may hold values from -0.1875 to 0.1875
- w_down: bfloat16 [1, 4864, 896], P(None, 'tp', ('fsdp', 'ctx')), may hold values from -0.078125 to 0.078125
Outputs:
- outputs: float32 [8, 2048, 896], P('fsdp', 'ctx')
- grad_inputs: float32 [8, 2048, 896], P('fsdp', 'ctx')
- grad_gains: float32 [1, 2, 896], P(None, None, ('fsdp', 'ctx'))
- grad_w_qkv: float32 [1, 896, 2, 576], P(None, ('fsdp', 'ctx'), 'tp')
- grad_b_qkv: float32 [1, 2, 9, 64], P(None, 'tp', None, ('fsdp', 'ctx'))
- grad_w_out: float32 [1, 2, 448, 896], P(None, 'tp', None, ('fsdp', 'ctx'))
- grad_w_gate_up: float32 [1, 896, 2, 4864], P(None, ('fsdp', 'ctx'), None, 'tp')
- grad_w_down: float32 [1, 4864, 896], P(None, 'tp', ('fsdp', 'ctx'))
Inputs may be any that keep to these rules, and one draw needn't show every extreme that they name: `block_order`: each row holds every number 0 to 31 once, and entries 2 c and 2 c + 1 of a row add up to 31.
All inputs are finite; a program needn't handle non-finite values.
Results may differ from a plain program's by a relative error of at most 0.019.
Values may be sent and summed in bfloat16 or wider, within the bound.
No kernel may reach another device: no remote copies, remote signals or barrier semaphores. Data moves between devices by JAX's collectives and lax.ppermute only.
A program may use at most 192 MiB of HBM per device.

v0:
```python
import math

import jax
import jax.numpy as jnp
from jax import lax
from jax.sharding import PartitionSpec as P

HEAD_DIM = 64


epsilon = 1e-06
rope_base = 1000000.0
masked_score = -1e30


def rms_forward(hidden, gain_vector):
    scale_rows = lax.rsqrt(jnp.mean(hidden * hidden, axis=-1, keepdims=True) + epsilon)
    unit_rows = hidden * scale_rows
    return (
        unit_rows,
        scale_rows,
        (unit_rows * gain_vector.astype(jnp.float32)).astype(jnp.bfloat16),
    )


def rms_backward(grad_normed, unit_rows, scale_rows, gain_vector):
    grad_gain = jnp.sum(grad_normed * unit_rows, axis=0)
    grad_unit = grad_normed * gain_vector.astype(jnp.float32)
    grad_hidden = scale_rows * (
        grad_unit - unit_rows * jnp.mean(grad_unit * unit_rows, axis=-1, keepdims=True)
    )
    return (grad_hidden, grad_gain)


def rotary(positions, head_width):
    half_dim = head_width // 2
    freq_steps = jnp.arange(half_dim, dtype=jnp.float32)
    frequency = jnp.exp(freq_steps * (-2.0 * math.log(rope_base) / head_width))
    angles = positions.astype(jnp.float32)[..., None] * frequency
    return (jnp.cos(angles), jnp.sin(angles))


def rotate(vectors, cosine, sine_table):
    half_dim = vectors.shape[-1] // 2
    first_half = vectors[..., :half_dim]
    second_half = vectors[..., half_dim:]
    return jnp.concatenate(
        [
            first_half * cosine - second_half * sine_table,
            second_half * cosine + first_half * sine_table,
        ],
        axis=-1,
    )


def rotate_back(vectors, cosine, sine_table):
    half_dim = vectors.shape[-1] // 2
    first_half = vectors[..., :half_dim]
    second_half = vectors[..., half_dim:]
    return jnp.concatenate(
        [
            first_half * cosine + second_half * sine_table,
            second_half * cosine - first_half * sine_table,
        ],
        axis=-1,
    )


def head_total(partial_rows):
    return lax.psum(partial_rows, "tp")


def feature_total(partial_rows):
    return lax.psum(partial_rows, "tp")


def unpack(gathered):
    return (
        gathered[0][:, 0, :],
        gathered[1][0].reshape(-1),
        gathered[2][0],
        gathered[3],
        gathered[4],
        gathered[5],
    )


def scores_of(query_rows, key_all, query_pos, key_pos):
    raw_scores = jnp.einsum(
        "sqkgd,slkd->skgql", query_rows, key_all, preferred_element_type=jnp.float32
    )
    raw_scores = raw_scores * (1.0 / math.sqrt(HEAD_DIM))
    allowed = key_pos[:, None, None, None, :] <= query_pos[:, None, None, :, None]
    return jnp.where(allowed, raw_scores, masked_score)


def layer_forward(flat_rows, weights, query_pos, key_pos, query_cos, query_sin):
    qkv_w, qkv_b, out_w, gate_up_w, down_w, gain_pair = weights
    seq_dev, local_rows = query_pos.shape
    q_width = out_w.shape[0]
    kv_here = (qkv_w.shape[1] - q_width) // (2 * HEAD_DIM)
    group_size = q_width // HEAD_DIM // kv_here
    first_unit, first_scale, first_normed = rms_forward(flat_rows, gain_pair[0])
    projected = jnp.dot(first_normed, qkv_w, preferred_element_type=jnp.float32) + qkv_b.astype(
        jnp.float32
    )
    query_raw = projected[:, :q_width].reshape(seq_dev, local_rows, kv_here, group_size, HEAD_DIM)
    key_raw = projected[:, q_width : q_width + kv_here * HEAD_DIM].reshape(
        seq_dev, local_rows, kv_here, HEAD_DIM
    )
    value_raw = projected[:, q_width + kv_here * HEAD_DIM :].reshape(
        seq_dev, local_rows, kv_here, HEAD_DIM
    )
    query_rows = rotate(
        query_raw, query_cos[:, :, None, None, :], query_sin[:, :, None, None, :]
    ).astype(jnp.bfloat16)
    key_rows = rotate(key_raw, query_cos[:, :, None, :], query_sin[:, :, None, :]).astype(
        jnp.bfloat16
    )
    pair_rows = jnp.concatenate([key_rows, value_raw.astype(jnp.bfloat16)], axis=-1)
    pair_rows = pair_rows.reshape(seq_dev, local_rows, kv_here * 2 * HEAD_DIM)
    gathered = lax.all_gather(pair_rows, "ctx", axis=1, tiled=True).reshape(
        seq_dev, -1, kv_here, 2 * HEAD_DIM
    )
    key_all = gathered[..., :HEAD_DIM]
    value_all = gathered[..., HEAD_DIM:]
    scores = scores_of(query_rows, key_all, query_pos, key_pos)
    row_top = jnp.max(scores, axis=-1, keepdims=True)
    log_total = row_top + jnp.log(jnp.sum(jnp.exp(scores - row_top), axis=-1, keepdims=True))
    probs_low = jnp.exp(scores - log_total).astype(jnp.bfloat16)
    attended = jnp.einsum(
        "skgql,slkd->sqkgd", probs_low, value_all, preferred_element_type=jnp.float32
    ).astype(jnp.bfloat16)
    token_count = seq_dev * local_rows
    mixed_rows = flat_rows + head_total(
        jnp.dot(attended.reshape(token_count, q_width), out_w, preferred_element_type=jnp.float32)
    )
    second_unit, second_scale, second_normed = rms_forward(mixed_rows, gain_pair[1])
    gate_up = jnp.einsum(
        "td,dcf->tcf", second_normed, gate_up_w, preferred_element_type=jnp.float32
    )
    gate_part = gate_up[:, 0, :]
    up_part = gate_up[:, 1, :]
    activated = (jax.nn.silu(gate_part) * up_part).astype(jnp.bfloat16)
    result_rows = mixed_rows + head_total(
        jnp.dot(activated, down_w, preferred_element_type=jnp.float32)
    )
    saved_state = (
        first_unit,
        first_scale,
        first_normed,
        query_rows,
        gathered,
        log_total,
        attended,
        second_unit,
        second_scale,
        second_normed,
        gate_part,
        up_part,
        activated,
    )
    return (result_rows, saved_state)


def layer_backward(gradient, saved_state, weights, query_pos, key_pos, query_cos, query_sin):
    qkv_w, qkv_b, out_w, gate_up_w, down_w, gain_pair = weights
    (
        first_unit,
        first_scale,
        first_normed,
        query_rows,
        gathered,
        log_total,
        attended,
        second_unit,
        second_scale,
        second_normed,
        gate_part,
        up_part,
        activated,
    ) = saved_state
    seq_dev, local_rows = query_pos.shape
    token_count = seq_dev * local_rows
    q_width = out_w.shape[0]
    kv_here = gathered.shape[2]
    key_all = gathered[..., :HEAD_DIM]
    value_all = gathered[..., HEAD_DIM:]
    grad_low = gradient.astype(jnp.bfloat16)
    grad_down = jnp.einsum("tf,td->fd", activated, grad_low, preferred_element_type=jnp.float32)
    d_activated = jnp.einsum("td,fd->tf", grad_low, down_w, preferred_element_type=jnp.float32)
    sigmoid_gate = jax.nn.sigmoid(gate_part)
    d_gate = d_activated * up_part * sigmoid_gate * (1.0 + gate_part * (1.0 - sigmoid_gate))
    d_up = d_activated * (gate_part * sigmoid_gate)
    d_gate_up = jnp.stack([d_gate, d_up], axis=1).astype(jnp.bfloat16)
    grad_gate_up = jnp.einsum(
        "td,tcf->dcf", second_normed, d_gate_up, preferred_element_type=jnp.float32
    )
    d_second = feature_total(
        jnp.einsum("tcf,dcf->td", d_gate_up, gate_up_w, preferred_element_type=jnp.float32)
    )
    d_middle, grad_gain_two = rms_backward(d_second, second_unit, second_scale, gain_pair[1])
    d_mixed = gradient + d_middle
    d_mixed_low = d_mixed.astype(jnp.bfloat16)
    grad_out = jnp.einsum(
        "tq,td->qd",
        attended.reshape(token_count, q_width),
        d_mixed_low,
        preferred_element_type=jnp.float32,
    )
    d_attended = jnp.einsum(
        "td,qd->tq", d_mixed_low, out_w, preferred_element_type=jnp.float32
    ).astype(jnp.bfloat16)
    d_attended = d_attended.reshape(attended.shape)
    scores = scores_of(query_rows, key_all, query_pos, key_pos)
    probs_full = jnp.exp(scores - log_total)
    probs_low = probs_full.astype(jnp.bfloat16)
    d_value_all = jnp.einsum(
        "skgql,sqkgd->slkd", probs_low, d_attended, preferred_element_type=jnp.float32
    )
    d_probs = jnp.einsum(
        "sqkgd,slkd->skgql", d_attended, value_all, preferred_element_type=jnp.float32
    )
    row_delta = jnp.sum(d_attended.astype(jnp.float32) * attended.astype(jnp.float32), axis=-1)
    row_delta = jnp.transpose(row_delta, (0, 2, 3, 1))[..., None]
    d_scores = (probs_full * (d_probs - row_delta) * (1.0 / math.sqrt(HEAD_DIM))).astype(
        jnp.bfloat16
    )
    d_query = jnp.einsum("skgql,slkd->sqkgd", d_scores, key_all, preferred_element_type=jnp.float32)
    d_key_all = jnp.einsum(
        "skgql,sqkgd->slkd", d_scores, query_rows, preferred_element_type=jnp.float32
    )
    d_pair_all = jnp.concatenate([d_key_all, d_value_all], axis=-1).reshape(
        seq_dev, -1, kv_here * 2 * HEAD_DIM
    )
    d_pair = (
        lax.psum_scatter(d_pair_all.astype(jnp.bfloat16), "ctx", scatter_dimension=1, tiled=True)
        .astype(jnp.float32)
        .reshape(seq_dev, local_rows, kv_here, 2 * HEAD_DIM)
    )
    d_key_local = rotate_back(
        d_pair[..., :HEAD_DIM], query_cos[:, :, None, :], query_sin[:, :, None, :]
    )
    d_value_local = d_pair[..., HEAD_DIM:]
    d_query_pre = rotate_back(
        d_query, query_cos[:, :, None, None, :], query_sin[:, :, None, None, :]
    )
    d_projected = jnp.concatenate(
        [
            d_query_pre.reshape(token_count, q_width),
            d_key_local.reshape(token_count, kv_here * HEAD_DIM),
            d_value_local.reshape(token_count, kv_here * HEAD_DIM),
        ],
        axis=1,
    )
    grad_bias = jnp.sum(d_projected, axis=0)
    d_projected_low = d_projected.astype(jnp.bfloat16)
    grad_qkv = jnp.einsum(
        "td,tc->dc", first_normed, d_projected_low, preferred_element_type=jnp.float32
    )
    d_first = feature_total(
        jnp.einsum("tc,dc->td", d_projected_low, qkv_w, preferred_element_type=jnp.float32)
    )
    d_lower, grad_gain_one = rms_backward(d_first, first_unit, first_scale, gain_pair[0])
    d_hidden = d_mixed + d_lower
    grad_terms = (
        grad_qkv,
        grad_bias,
        grad_out,
        grad_gate_up,
        grad_down,
        jnp.stack([grad_gain_one, grad_gain_two]),
    )
    return (d_hidden, grad_terms)


def owner_sums(grad_terms):
    grad_qkv, grad_bias, grad_out, grad_gate_up, grad_down, gain_stack = grad_terms
    head_slots = grad_bias.shape[0] // HEAD_DIM
    row_parts = (
        lax.all_to_all(
            grad_qkv[None, :, None, :].astype(jnp.bfloat16),
            ("fsdp", "ctx"),
            split_axis=1,
            concat_axis=0,
            tiled=True,
        ).astype(jnp.float32),
        lax.all_to_all(
            grad_gate_up[None].astype(jnp.bfloat16),
            ("fsdp", "ctx"),
            split_axis=1,
            concat_axis=0,
            tiled=True,
        ).astype(jnp.float32),
    )
    column_parts = (
        lax.all_to_all(
            grad_bias.reshape(head_slots, HEAD_DIM)[None].astype(jnp.bfloat16),
            ("fsdp", "ctx"),
            split_axis=2,
            concat_axis=0,
            tiled=True,
        ).astype(jnp.float32),
        lax.all_to_all(
            grad_out[None].astype(jnp.bfloat16),
            ("fsdp", "ctx"),
            split_axis=2,
            concat_axis=0,
            tiled=True,
        ).astype(jnp.float32),
        lax.all_to_all(
            grad_down[None].astype(jnp.bfloat16),
            ("fsdp", "ctx"),
            split_axis=2,
            concat_axis=0,
            tiled=True,
        ).astype(jnp.float32),
        lax.all_to_all(
            gain_stack[None].astype(jnp.bfloat16),
            ("fsdp", "ctx"),
            split_axis=2,
            concat_axis=0,
            tiled=True,
        ).astype(jnp.float32),
    )
    return (
        jnp.sum(row_parts[0], axis=0),
        jnp.sum(column_parts[0], axis=0)[None],
        jnp.sum(column_parts[1], axis=0)[None],
        jnp.sum(row_parts[1], axis=0),
        jnp.sum(column_parts[2], axis=0),
        jnp.sum(column_parts[3], axis=0),
    )


def body(inputs, block_order, cotangent, gains, w_qkv, b_qkv, w_out, w_gate_up, w_down):
    seq_dev, local_rows, model_width = inputs.shape
    layers = gains.shape[0]
    block_len = local_rows // 2
    context_index = lax.axis_index("ctx")
    own_blocks = lax.dynamic_slice_in_dim(block_order, 2 * context_index, 2, 1)
    offsets = jnp.arange(block_len, dtype=jnp.int32)
    query_pos = (own_blocks[:, :, None] * block_len + offsets).reshape(seq_dev, local_rows)
    key_pos = (block_order[:, :, None] * block_len + offsets).reshape(seq_dev, -1)
    query_cos, query_sin = rotary(query_pos, HEAD_DIM)
    hidden = inputs.reshape(seq_dev * local_rows, model_width)
    kept_weights = []
    layer_index = 0
    weights = unpack(
        (
            lax.all_gather(w_qkv[layer_index], ("fsdp", "ctx"), axis=0, tiled=True),
            lax.all_gather(b_qkv[layer_index], ("fsdp", "ctx"), axis=2, tiled=True),
            lax.all_gather(w_out[layer_index], ("fsdp", "ctx"), axis=2, tiled=True),
            lax.all_gather(w_gate_up[layer_index], ("fsdp", "ctx"), axis=0, tiled=True),
            lax.all_gather(w_down[layer_index], ("fsdp", "ctx"), axis=1, tiled=True),
            lax.all_gather(gains[layer_index], ("fsdp", "ctx"), axis=1, tiled=True),
        )
    )
    hidden, saved_state = layer_forward(hidden, weights, query_pos, key_pos, query_cos, query_sin)
    kept_weights.append(weights)
    kept_state = [saved_state]
    outputs = hidden.reshape(seq_dev, local_rows, model_width)
    gradient = cotangent.reshape(seq_dev * local_rows, model_width)
    layer_terms = [None] * layers
    for layer_index in reversed(range(layers)):
        weights = unpack(
            (
                lax.all_gather(w_qkv[layer_index], ("fsdp", "ctx"), axis=0, tiled=True),
                lax.all_gather(b_qkv[layer_index], ("fsdp", "ctx"), axis=2, tiled=True),
                lax.all_gather(w_out[layer_index], ("fsdp", "ctx"), axis=2, tiled=True),
                lax.all_gather(w_gate_up[layer_index], ("fsdp", "ctx"), axis=0, tiled=True),
                lax.all_gather(w_down[layer_index], ("fsdp", "ctx"), axis=1, tiled=True),
                lax.all_gather(gains[layer_index], ("fsdp", "ctx"), axis=1, tiled=True),
            )
        )
        gradient, grad_terms = layer_backward(
            gradient, kept_state[layer_index], weights, query_pos, key_pos, query_cos, query_sin
        )
        layer_terms[layer_index] = owner_sums(grad_terms)
    summed = [jnp.stack([layer_terms[0][member_index]]) for member_index in range(6)]
    grad_inputs = gradient.reshape(seq_dev, local_rows, model_width)
    return (outputs, grad_inputs, summed[5], summed[0], summed[1], summed[2], summed[3], summed[4])


def solution(mesh):
    in_specs = (
        P("fsdp", "ctx", None),
        P("fsdp", None),
        P("fsdp", "ctx", None),
        P(None, None, ("fsdp", "ctx")),
        P(None, ("fsdp", "ctx"), "tp", None),
        P(None, "tp", None, ("fsdp", "ctx")),
        P(None, "tp", None, ("fsdp", "ctx")),
        P(None, ("fsdp", "ctx"), None, "tp"),
        P(None, "tp", ("fsdp", "ctx")),
    )
    out_specs = (
        P("fsdp", "ctx", None),
        P("fsdp", "ctx", None),
        P(None, None, ("fsdp", "ctx")),
        P(None, ("fsdp", "ctx"), "tp", None),
        P(None, "tp", None, ("fsdp", "ctx")),
        P(None, "tp", None, ("fsdp", "ctx")),
        P(None, ("fsdp", "ctx"), None, "tp"),
        P(None, "tp", ("fsdp", "ctx")),
    )
    return jax.shard_map(body, mesh=mesh, in_specs=in_specs, out_specs=out_specs, check_vma=False)
```

profile of v0, /device:TPU:68, one launch (start us, length us, event | category | flops | bytes accessed | tf_op | source)
XLA Modules:
  0.0 1454.1 jit_solution(14438663603092770260)
XLA Ops:
  8.9 152.6 %all-gather = bf16[1,2,896]{1,0,2:T(2,128)(2,1)S(1)} all-gather(bf16[1,2,14]{1,0,2:T(2,128)(2,1)S(1)} %copy.118), channel_id=2, replica_groups=mesh['fsdp'=4,'ctx'=16,'tp'=2] {'fsdp','ctx'}, dimensions={2}, use_global_device_ids=true | all-gather | bytes 3640 | tf_op jit(solution)/shard_map/all_gather | solution.py:356
  169.6 191.8 %all-gather.1 = bf16[1,896,1,576]{3,2,0,1:T(2,128)(2,1)} all-gather(bf16[1,14,1,576]{3,2,0,1:T(2,128)(2,1)S(1)} %copy.119), channel_id=3, replica_groups=mesh['fsdp'=4,'ctx'=16,'tp'=2] {'fsdp','ctx'}, dimensions={1}, use_global_device_ids=true | all-gather | bytes 1048320 | tf_op jit(solution)/shard_map/all_gather | solution.py:351
  366.1 170.7 %all-gather.2 = bf16[1,1,9,64]{2,1,0,3:T(2,128)(2,1)S(1)} all-gather(bf16[1,1,9,1]{2,1,0,3:T(2,128)(2,1)S(1)} %bitcast.295), channel_id=4, replica_groups=mesh['fsdp'=4,'ctx'=16,'tp'=2] {'fsdp','ctx'}, dimensions={3}, use_global_device_ids=true | all-gather | bytes 1170 | tf_op jit(solution)/shard_map/all_gather | solution.py:352
  539.1 189.4 %all-gather.4 = bf16[1,1,448,896]{2,1,0,3:T(2,128)(2,1)} all-gather(bf16[1,1,448,14]{2,1,0,3:T(2,128)(2,1)S(1)} %copy.130), channel_id=6, replica_groups=mesh['fsdp'=4,'ctx'=16,'tp'=2] {'fsdp','ctx'}, dimensions={3}, use_global_device_ids=true | all-gather | bytes 815360 | tf_op jit(solution)/shard_map/all_gather | solution.py:353
  734.9 8.4 fusion.4
  743.4 8.2 exponential_reduce_fusion
  764.5 45.0 %all-reduce.5.cloned.1.call-done = f32[256,896]{1,0:T(8,128)} async-done(((f32[256,896]{1,0:T(8,128)}), f32[256,896]{1,0:T(8,128)}) %all-reduce.5.cloned.1.call-update) | async-done | bytes 917520 | tf_op jit(solution)/shard_map/psum | solution.py:70
  810.8 56.9 %all-gather.15.cloned.1.call-done = bf16[1,2432,896]{1,0,2:T(2,128)(2,1)} async-done(((bf16[1,2432,14]{1,0,2:T(2,128)(2,1)}), bf16[1,2432,896]{1,0,2:T(2,128)(2,1)}) %all-gather.15.cloned.1.call-update) | async-done | bytes 4358160 | tf_op jit(solution)/shard_map/all_gather | solution.py:355
  867.7 18.5 %copy.135 = bf16[1,2432,896]{2,1,0:T(8,128)(2,1)} copy(bf16[1,2432,896]{1,0,2:T(2,128)(2,1)} %all-gather.15.cloned.1.call-done) | data formatting | bytes 8716288 | tf_op jit(solution)/shard_map/all_gather | solution.py:355
  886.2 64.1 %all-gather.13.cloned.1.call-done = bf16[1,896,2,2432]{3,2,0,1:T(2,128)(2,1)} async-done(((bf16[1,14,2,2432]{3,2,0,1:T(2,128)(2,1)}), bf16[1,896,2,2432]{3,2,0,1:T(2,128)(2,1)}) %all-gather.13.cloned.1.call-update) | async-done | bytes 8716304 | tf_op jit(solution)/shard_map/all_gather | solution.py:354
  964.3 25.5 %all-reduce.7.cloned.1.call-done = f32[256,896]{1,0:T(8,128)} async-done(((f32[256,896]{1,0:T(8,128)}), f32[256,896]{1,0:T(8,128)}) %all-reduce.7.cloned.1.call-update) | async-done | bytes 917520 | tf_op jit(solution)/shard_map/psum | solution.py:74
  998.1 8.9 fusion.28
  1007.1 8.7 fusion.12
  1038.5 8.3 reduce.32
  1050.6 10.4 all-to-all-start.3
  1062.0 43.2 %reduce-scatter.4.cloned.1.call-done = bf16[128,256]{1,0:T(8,128)(2,1)} async-done(((bf16[2048,256]{1,0:T(8,128)(2,1)}), bf16[128,256]{1,0:T(8,128)(2,1)}) %reduce-scatter.4.cloned.1.call-update) | async-done | bytes 65552
  1107.7 10.2 all-to-all-start.2
  1124.1 18.9 %copy.152 = bf16[1,2432,896]{1,0,2:T(2,128)(2,1)} copy(bf16[1,2432,896]{2,1,0:T(8,128)(2,1)} %fusion.13) | data formatting | bytes 8716288 | tf_op jit(solution)/shard_map/convert_element_type | solution.py:312
  1143.0 28.6 %reduce.33 = bf16[896,2432]{1,0:T(8,128)(2,1)} reduce(bf16[896,1,2432]{2,1,0:T(2,128)(2,1)} %bitcast.276, bf16[]{:T(256)} %broadcast.190), dimensions={1}, to_apply=%bitcast.259.reduce_sub_computation | reduce | bytes 8716290
  1178.8 10.5 all-to-all-start.5
  1197.6 28.0 %all-reduce.9.cloned.1.call-done = (f32[256,896]{1,0:T(8,128)}, f32[256,896]{1,0:T(8,128)}) async-done(((f32[256,896]{1,0:T(8,128)}, f32[256,896]{1,0:T(8,128)}), (f32[256,896]{1,0:T(8,128)}, f32[256,896]{1,0:T(8,128)})) %all-reduce.9.cloned.1.call-update) | async-done | bytes 1835024 | tf_op jit(solution)/shard_map/psum | solution.py:70
  1229.1 8.9 all-to-all-done.5
  1238.0 9.8 all-to-all-start
  1255.9 9.9 reduce.31
  1269.0 10.8 all-to-all-start.1
  1284.0 25.3 %copy.151 = bf16[1,896,2,2432]{3,2,0,1:T(2,128)(2,1)} copy(bf16[1,896,2,2432]{3,1,2,0:T(8,128)(2,1)S(1)} %convert_bitcast_fusion) | data formatting | bytes 17432576 | tf_op jit(solution)/shard_map/convert_element_type | solution.py:289
  1309.3 10.5 all-to-all-start.4
  1326.4 7.9 convert_reduce_fusion.3
  1340.0 21.6 %reshape.501 = bf16[896,1,2432]{2,1,0:T(2,128)(2,1)} reshape(bf16[64,2,17024]{2,1,0:T(2,128)(2,1)} %all-to-all-done.5) | data formatting | bytes 8716288
  1361.6 30.1 %convert_reduce_fusion.1 = f32[2432,896]{0,1:T(8,128)} fusion(bf16[896,1,2432]{2,1,0:T(2,128)(2,1)} %reshape.501), kind=kLoop, calls=%fused_computation.14 | loop fusion | flops 2179072 | bytes 13074432 | tf_op jit(solution)/shard_map/convert_element_type | solution.py:317
  1391.7 9.5 reshape.462
  1437.2 9.5 convert_reduce_fusion
  (220 shorter events, 177.0 us)
Async XLA Ops:
  8.0 529.0 %copy-start.1 = (f32[2,128,896]{2,1,0:T(8,128)S(1)}, f32[2,128,896]{2,1,0:T(8,128)}, u32[]{:S(2)}) copy-start(f32[2,128,896]{2,1,0:T(8,128)} %param.9) | copy-start | bytes 2752516
  8.0 358.1 %copy-start.37 = (bf16[1,1,9,1]{2,3,1,0:T(2,128)(2,1)S(1)}, bf16[1,1,9,1]{2,3,1,0:T(2,128)(2,1)}, u32[]{:S(2)}) copy-start(bf16[1,1,9,1]{2,3,1,0:T(2,128)(2,1)} %param.14) | copy-start | bytes 58
  8.0 726.9 %all-gather.11.cloned.1.call-start = ((), (), s32[]{:S(2)}) async-start(), calls=%async_computation.9 | async-start | bytes 1114112 | tf_op jit(solution)/shard_map/all_gather | solution.py:122
  167.0 370.2 %copy-start.23 = (f32[896]{0:T(1024)}, f32[896]{0:T(1024)S(1)}, u32[]{:S(2)}) copy-start(f32[896]{0:T(1024)S(1)} %get-tuple-element.13) | copy-start | bytes 10756
  167.0 824.9 %copy-start.25 = (f32[896]{0:T(1024)}, f32[896]{0:T(1024)S(1)}, u32[]{:S(2)}) copy-start(f32[896]{0:T(1024)S(1)} %get-tuple-element.12) | copy-start | bytes 10756
  169.6 368.2 %copy-start.36 = (s32[2,32]{1,0:T(2,128)S(1)}, s32[2,32]{1,0:T(2,128)}, u32[]{:S(2)}) copy-start(s32[2,32]{1,0:T(2,128)} %param.10) | copy-start | bytes 772
  361.4 177.7 %copy-start.29 = (bf16[1,1,448,14]{2,3,1,0:T(8,128)(2,1)S(1)}, bf16[1,1,448,14]{2,3,1,0:T(8,128)(2,1)}, u32[]{:S(2)}) copy-start(bf16[1,1,448,14]{2,3,1,0:T(8,128)(2,1)} %param.15) | copy-start | bytes 37636
  366.1 367.0 %copy-start.2 = (bf16[1,896,1,576]{1,3,2,0:T(8,128)(2,1)}, bf16[1,896,1,576]{1,3,2,0:T(8,128)(2,1)S(1)}, u32[]{:S(2)}) copy-start(bf16[1,896,1,576]{1,3,2,0:T(8,128)(2,1)S(1)} %copy.120) | copy-start | bytes 3096580
  537.7 196.1 %copy-start.34 = (f32[32]{0:T(128)}, f32[32]{0:T(128)S(1)}, u32[]{:S(2)}) copy-start(f32[32]{0:T(128)S(1)} %multiply_exponential_fusion) | copy-start | bytes 388
  538.2 195.7 %copy-start.27 = (f32[2,128]{1,0:T(2,128)}, f32[2,128]{1,0:T(2,128)S(1)}, u32[]{:S(2)}) copy-start(f32[2,128]{1,0:T(2,128)S(1)} %get-tuple-element.18) | copy-start | bytes 3076
  539.1 270.4 %all-reduce.5.cloned.1.call-start = ((), (), s32[]{:S(2)}) async-start(), calls=%async_computation.7 | async-start | bytes 1835008 | tf_op jit(solution)/shard_map/psum | solution.py:70
  733.1 26.6 %copy-start.4 = (bf16[1,1,448,896]{3,2,1,0:T(8,128)(2,1)}, bf16[1,1,448,896]{3,2,1,0:T(8,128)(2,1)S(1)}, u32[]{:S(2)}) copy-start(bf16[1,1,448,896]{3,2,1,0:T(8,128)(2,1)S(1)} %copy.131) | copy-start | bytes 2408452
  761.7 106.0 %all-gather.15.cloned.1.call-start = ((), (), s32[]{:S(2)}) async-start(), calls=%async_computation.11 | async-start | bytes 8852480 | tf_op jit(solution)/shard_map/all_gather | solution.py:355
  762.6 187.8 %all-gather.13.cloned.1.call-start = ((), (), s32[]{:S(2)}) async-start(), calls=%async_computation.10 | async-start | bytes 8852480 | tf_op jit(solution)/shard_map/all_gather | solution.py:354
  763.2 226.6 %all-reduce.7.cloned.1.call-start = ((), (), s32[]{:S(2)}) async-start(), calls=%async_computation.8 | async-start | bytes 1835008 | tf_op jit(solution)/shard_map/psum | solution.py:74
  810.8 181.1 %copy-start.30 = (f32[256]{0:T(256)}, f32[256]{0:T(256)S(1)}, u32[]{:S(2)}) copy-start(f32[256]{0:T(256)S(1)} %add_rsqrt_fusion) | copy-start | bytes 3076
  964.3 141.0 %reduce-scatter.4.cloned.1.call-start = ((), (), s32[]{:S(2)}) async-start(), calls=%async_computation.12 | async-start | bytes 1114112
  1007.0 11.6 copy-start.14
  1007.0 11.6 copy-start.16
  1038.0 68.3 %copy-start.28 = (f32[2,128]{1,0:T(2,128)S(1)}, f32[2,128]{1,0:T(2,128)}, u32[]{:S(2)}) copy-start(f32[2,128]{1,0:T(2,128)} %copy-done.27) | copy-start | bytes 3076
  1038.0 68.3 %copy-start.35 = (f32[32]{0:T(128)S(1)}, f32[32]{0:T(128)}, u32[]{:S(2)}) copy-start(f32[32]{0:T(128)} %copy-done.34) | copy-start | bytes 388
  1050.6 57.1 %all-to-all-start.3 = ((bf16[64,2,3136]{2,1,0:T(2,128)(2,1)}), bf16[64,2,3136]{2,1,0:T(2,128)(2,1)}, u32[]{:S(2)}, u32[]{:S(2)}) async-start(bf16[64,2,3136]{2,1,0:T(2,128)(2,1)} %reshape.498), calls=%async_computation.3 | async-start | bytes 1638400 | tf_op jit(solution)/shard_map/all_to_all | solution.py:304
  1107.7 71.2 %all-to-all-start.2 = ((bf16[1,9,64]{1,0,2:T(2,128)(2,1)}), bf16[1,9,64]{1,0,2:T(2,128)(2,1)S(1)}, u32[]{:S(2)}, u32[]{:S(2)}) async-start(bf16[1,9,64]{1,0,2:T(2,128)(2,1)} %copy.148), calls=%async_computation.2 | async-start | bytes 65536 | tf_op jit(solution)/shard_map/all_to_all | solution.py:297
  1178.8 59.2 %all-to-all-start.5 = ((bf16[64,2,17024]{2,1,0:T(2,128)(2,1)}), bf16[64,2,17024]{2,1,0:T(2,128)(2,1)}, u32[]{:S(2)}, u32[]{:S(2)}) async-start(bf16[64,2,17024]{2,1,0:T(2,128)(2,1)} %reshape.500), calls=%async_computation.5 | async-start | bytes 8716288 | tf_op jit(solution)/shard_map/all_to_all | solution.py:311
  1189.3 36.3 %all-reduce.9.cloned.1.call-start = ((), (), s32[]{:S(2)}) async-start(), calls=%async_computation.13 | async-start | bytes 3670016 | tf_op jit(solution)/shard_map/psum | solution.py:70
  1196.1 29.6 %copy-start.24 = (f32[896]{0:T(1024)S(1)}, f32[896]{0:T(1024)}, u32[]{:S(2)}) copy-start(f32[896]{0:T(1024)} %copy-done.23) | copy-start | bytes 10756
  1196.1 29.6 %copy-start.32 = (f32[256]{0:T(256)S(1)}, f32[256]{0:T(256)}, u32[]{:S(2)}) copy-start(f32[256]{0:T(256)} %get-tuple-element.39) | copy-start | bytes 3076
  1238.0 31.0 %all-to-all-start = ((bf16[1,2,896]{1,0,2:T(2,128)(2,1)}), bf16[1,2,896]{1,0,2:T(2,128)(2,1)}, u32[]{:S(2)}, u32[]{:S(2)}) async-start(bf16[1,2,896]{1,0,2:T(2,128)(2,1)} %copy.145), calls=%async_computation | async-start | bytes 917504 | tf_op jit(solution)/shard_map/all_to_all | solution.py:318
  1255.9 23.8 %copy-start.26 = (f32[896]{0:T(1024)S(1)}, f32[896]{0:T(1024)}, u32[]{:S(2)}) copy-start(f32[896]{0:T(1024)} %copy-done.25) | copy-start | bytes 10756
  1255.9 23.8 %copy-start.31 = (f32[256]{0:T(256)S(1)}, f32[256]{0:T(256)}, u32[]{:S(2)}) copy-start(f32[256]{0:T(256)} %copy-done.30) | copy-start | bytes 3076
  1269.0 40.3 %all-to-all-start.1 = ((bf16[64,2,4032]{2,1,0:T(2,128)(2,1)}), bf16[64,2,4032]{2,1,0:T(2,128)(2,1)}, u32[]{:S(2)}, u32[]{:S(2)}) async-start(bf16[64,2,4032]{2,1,0:T(2,128)(2,1)} %reshape.496), calls=%async_computation.1 | async-start | bytes 2097152 | tf_op jit(solution)/shard_map/all_to_all | solution.py:281
  1309.3 127.9 %all-to-all-start.4 = ((bf16[1,896,2,2432]{3,2,0,1:T(2,128)(2,1)}), bf16[1,896,2,2432]{3,2,0,1:T(2,128)(2,1)}, u32[]{:S(2)}, u32[]{:S(2)}) async-start(bf16[1,896,2,2432]{3,2,0,1:T(2,128)(2,1)} %copy.151), calls=%async_computation.4 | async-start | bytes 17432576 | tf_op jit(solution)/shard_map/all_to_all | solution.py:288
  (23 other events, 133.2 us)
Sparse Core Ops, SparseCore 0:
  539.2 63.0 all-gather.10
  761.9 47.5 all-reduce.4
  964.4 25.3 all-reduce.6
  1028.2 76.9 reduce-scatter.3
  1197.7 27.9 all-reduce.8
Sparse Core Ops, SparseCore 1:
  766.0 101.6 all-gather.14
  870.8 79.5 all-gather.12
where the time goes:
time: 1460 us; the launch traced here: 1450 us
  blocking collectives  705 us (48%)
  waiting for transfers between devices  279 us (19%)
  local copies, waits for them, and re-layouts  171 us (12%)
  other arithmetic  143 us (10%)
  matrix products  76.8 us (5%)
  starting transfers between devices  63.1 us (4%)
  between operations  16.3 us (1%)
    all_gather x1, blocking collectives, body(): lax.all_gather(w_qkv[layer_index], ('fsdp', 'ctx'), axis=0, tiled=True)  192 us
    all_gather x1, blocking collectives, body(): lax.all_gather(w_out[layer_index], ('fsdp', 'ctx'), axis=2, tiled=True)  189 us
    all_gather x1, blocking collectives, body(): lax.all_gather(b_qkv[layer_index], ('fsdp', 'ctx'), axis=2, tiled=True)  171 us
    all_gather x1, blocking collectives, body(): lax.all_gather(gains[layer_index], ('fsdp', 'ctx'), axis=1, tiled=True)  153 us
    psum x2, waiting for transfers between devices, head_total(): return lax.psum(partial_rows, 'tp')  73 us
    unnamed x101, local copies, waits for them, and re-layouts  66.2 us
    all_gather x1, waiting for transfers between devices, body(): lax.all_gather(w_gate_up[layer_index], ('fsdp', 'ctx'), axis=0, tiled=True)  64.1 us
    all_gather x1, waiting for transfers between devices, body(): lax.all_gather(w_down[layer_index], ('fsdp', 'ctx'), axis=1, tiled=True)  56.9 us
  transfers between devices with their start and end apart: 13, of which 8 were waited for; matrix products, arithmetic and copies ran while one was open for 20% of the time, Pallas kernels for 0%

commit v1 on v0

v1 whole, which is shorter than its diff:
```python
import math

import jax
import jax.numpy as jnp
from jax import lax
from jax.experimental import pallas as pl
from jax.experimental.pallas import tpu as pltpu
from jax.sharding import PartitionSpec as P

HD = 64
EPS = 1e-06
ROPE_BASE = 1000000.0
MASKED = -1e30
ROWS = 14
SLOT = 16
DM = 896
DP = 1024
OWNERS = 64
FFB = 640
CH = 256
GRP = ("fsdp", "ctx")
BF = jnp.bfloat16
F32 = jnp.float32
NT = (((1,), (1,)), ((), ()))
TN = (((0,), (0,)), ((), ()))
VMEM_ALL = pl.BlockSpec(memory_space=pltpu.VMEM)
PARAMS = pltpu.CompilerParams(vmem_limit_bytes=56 << 20)


def dot(a, b):
    return jnp.dot(a, b, preferred_element_type=F32)


def dotd(a, b, dims):
    return lax.dot_general(a, b, dims, preferred_element_type=F32)


def low(v):
    return lax.reduce_precision(v, 8, 7)


def selection():
    d = lax.broadcasted_iota(jnp.int32, (DM, DP), 0)
    p = lax.broadcasted_iota(jnp.int32, (DM, DP), 1)
    return ((d // ROWS) * SLOT + d % ROWS == p).astype(BF)


def split3(v):
    hi = low(v)
    rest = v - hi
    mid = low(rest)
    tail = rest - mid
    return jnp.concatenate([hi.astype(BF), mid.astype(BF), tail.astype(BF)], axis=0)


def sum3(v):
    n = v.shape[0] // 3
    return (v[:n] + v[n : 2 * n]) + v[2 * n :]


def pad_features(v, sel):
    return sum3(dot(split3(v), sel))


def unpad_features(v, sel):
    return sum3(dotd(split3(v), sel, NT))


def spread(v, count, axes):
    full = jnp.broadcast_to(v[None], (count,) + v.shape)
    return lax.all_to_all(full, axes, split_axis=0, concat_axis=0, tiled=True)


def swap_tp(v):
    return lax.ppermute(v, "tp", [(0, 1), (1, 0)])


def lanes(shape):
    return lax.broadcasted_iota(jnp.int32, shape, len(shape) - 1)


def half_swap(v, lane):
    return jnp.where(lane % HD < HD // 2, pltpu.roll(v, 96, 1), pltpu.roll(v, 32, 1))


def qkv_kernel(x_ref, w_ref, cos_ref, sin_ref, q_ref, kv_ref, n_ref, g_ref):
    x = x_ref[...]
    scale = lax.rsqrt(jnp.sum(x * x, axis=-1, keepdims=True) * (1.0 / DM) + EPS)
    pick = (
        lax.broadcasted_iota(jnp.int32, (8, 128), 0) + HD
        == lax.broadcasted_iota(jnp.int32, (8, 128), 1)
    ) & (lax.broadcasted_iota(jnp.int32, (8, 128), 0) < 2)
    gain_rows = dotd(jnp.where(pick, 1.0, 0.0).astype(BF), w_ref[:, 512:640], NT)
    g_ref[...] = gain_rows
    wide = lanes(x.shape)
    normed = jnp.where(wide % SLOT == ROWS, 1.0, x * scale * gain_rows[0:1]).astype(BF)
    n_ref[...] = normed
    proj = dot(normed, w_ref[...])
    cosine = cos_ref[...]
    sine = sin_ref[...]
    lane = lanes(cosine.shape)
    left = lane < HD
    rots = []
    for g in range(4):
        v = proj[:, g * 128 : g * 128 + 128]
        rots.append(v * cosine + half_swap(v, lane) * sine)
    for h in range(7):
        r = rots[h // 2]
        if h % 2:
            r = pltpu.roll(r, HD, 1)
        qh = jnp.where(left, r * 0.125, 0.0).astype(BF)
        for s in range(2):
            for b in range(2):
                q_ref[s, b, h * 64 : h * 64 + 64, :] = qh[s * 128 + b * 64 : s * 128 + b * 64 + 64]
    pair = jnp.where(
        left, pltpu.roll(rots[3], HD, 1), pltpu.roll(proj[:, 512:640], HD, 1)
    ).astype(BF)
    for c in range(kv_ref.shape[0]):
        kv_ref[c] = pair


def order_rows(bo_ref, s, kv_ref, kvs):
    for j in range(32):
        at = pl.multiple_of(bo_ref[s, j] * 64, 64)
        kvs[pl.ds(at, 64), :] = kv_ref[j // 2, 0, (j % 2) * 64 : (j % 2) * 64 + 64, :]


def allowed(block, j):
    key = j * CH + lax.broadcasted_iota(jnp.int32, (448, CH), 1)
    query = block * 64 + lax.broadcasted_iota(jnp.int32, (448, CH), 0) % 64
    return key <= query


def attn_fwd_kernel(bo_ref, own_ref, q_ref, kv_ref, att_ref, lse_ref, kvs, sbuf, mbuf, lbuf, obuf):
    s = pl.program_id(0)
    order_rows(bo_ref, s, kv_ref, kvs)
    for b in range(2):
        block = own_ref[s, b]
        count = block // 4 + 1
        q = q_ref[0, b]
        mbuf[...] = jnp.full(mbuf.shape, MASKED, F32)

        def first(j, carry):
            k = kvs[pl.ds(pl.multiple_of(j * CH, CH), CH), :]
            sc = jnp.where(allowed(block, j), dotd(q, k, NT), MASKED)
            sbuf[j] = sc
            mbuf[...] = jnp.maximum(mbuf[...], jnp.maximum(sc[:, :128], sc[:, 128:]))
            return carry

        lax.fori_loop(0, count, first, 0)
        top = jnp.max(mbuf[...], axis=-1, keepdims=True)
        lbuf[...] = jnp.zeros(lbuf.shape, F32)
        obuf[...] = jnp.zeros(obuf.shape, F32)

        def second(j, carry):
            k = kvs[pl.ds(pl.multiple_of(j * CH, CH), CH), :]
            p = jnp.exp(sbuf[j] - top)
            lbuf[...] += p[:, :128] + p[:, 128:]
            obuf[...] += dot(p.astype(BF), k)
            return carry

        lax.fori_loop(0, count, second, 0)
        total = jnp.sum(lbuf[...], axis=-1, keepdims=True)
        lse_ref[0, b] = jnp.broadcast_to(top + jnp.log(total), (448, 128))
        o = obuf[...] / total
        left = lanes((64, 128)) < HD
        for g in range(4):
            even = pltpu.roll(o[g * 128 : g * 128 + 64], HD, 1)
            odd = o[g * 128 + 64 : g * 128 + 128] if g < 3 else jnp.zeros((64, 128), F32)
            att_ref[0, b * 64 : b * 64 + 64, g * 128 : g * 128 + 128] = jnp.where(
                left, even, odd
            ).astype(BF)


def head_rows(ref, b):
    right = lanes((64, 128)) >= HD
    parts = []
    for h in range(7):
        g = h // 2
        v = ref[0, b * 64 : b * 64 + 64, g * 128 : g * 128 + 128].astype(F32)
        if h % 2 == 0:
            v = pltpu.roll(v, HD, 1)
        parts.append(jnp.where(right, v, 0.0))
    return jnp.concatenate(parts, axis=0)


def attn_bwd_kernel(
    bo_ref, own_ref, q_ref, kv_ref, att_ref, do_ref, lse_ref, dq_ref, dkv_ref, kvs, dkvs, dqb
):
    s = pl.program_id(0)
    order_rows(bo_ref, s, kv_ref, kvs)
    dkvs[...] = jnp.zeros(dkvs.shape, F32)
    for b in range(2):
        block = own_ref[s, b]
        count = block // 4 + 1
        q = q_ref[0, b]
        do32 = head_rows(do_ref, b)
        delta = jnp.sum(do32 * head_rows(att_ref, b), axis=-1, keepdims=True)
        do = do32.astype(BF)
        lse = lse_ref[0, b][:, 0:1]
        dqb[...] = jnp.zeros(dqb.shape, F32)

        def step(j, carry):
            at = pl.ds(pl.multiple_of(j * CH, CH), CH)
            k = kvs[at, :]
            p = jnp.where(allowed(block, j), jnp.exp(dotd(q, k, NT) - lse), 0.0)
            ds = (p * (dotd(do, k, NT) - delta)).astype(BF)
            dqb[...] += dot(ds, k)
            dkvs[at, :] += dotd(ds, q, TN) + dotd(p.astype(BF), do, TN)
            return carry

        lax.fori_loop(0, count, step, 0)
        dq_ref[0, b] = dqb[...] * 0.125
    for j in range(32):
        at = pl.multiple_of(bo_ref[s, j] * 64, 64)
        dkv_ref[j // 2, 0, (j % 2) * 64 : (j % 2) * 64 + 64, :] = dkvs[pl.ds(at, 64), :].astype(BF)


def dproj_kernel(dq_ref, dkv_ref, cos_ref, sin_ref, w_ref, dp_ref, dn_ref):
    dkv = dkv_ref[0].astype(F32)
    for c in range(1, dkv_ref.shape[0]):
        dkv = dkv + dkv_ref[c].astype(F32)
    cosine = cos_ref[...]
    sine = sin_ref[...]
    lane = lanes(cosine.shape)
    left = lane < HD

    def head(h):
        return jnp.concatenate(
            [dq_ref[s, b, h * 64 : h * 64 + 64, :] for s in range(2) for b in range(2)], axis=0
        )

    for g in range(4):
        odd = head(2 * g + 1) if g < 3 else dkv
        u = jnp.where(left, head(2 * g), pltpu.roll(odd, HD, 1))
        dp_ref[:, g * 128 : g * 128 + 128] = (u * cosine - half_swap(u, lane) * sine).astype(BF)
    dp_ref[:, 512:640] = jnp.where(left, pltpu.roll(dkv, HD, 1), 0.0).astype(BF)
    dn_ref[...] = dotd(dp_ref[...], w_ref[...], NT)


def mlp_kernel(n_ref, dm_ref, w_ref, act_ref, dg_ref, du_ref, dn_ref, out_ref):
    n = n_ref[...]
    gate = dot(n, w_ref[:, 0:FFB])
    up = dot(n, w_ref[:, FFB : 2 * FFB])
    dact = dot(dm_ref[...], w_ref[:, 2 * FFB : 3 * FFB])
    sg = 1.0 / (1.0 + jnp.exp(-gate))
    silu = gate * sg
    act = (silu * up).astype(BF)
    dg = (dact * up * sg * (1.0 + gate * (1.0 - sg))).astype(BF)
    du = (dact * silu).astype(BF)
    act_ref[...] = act
    dg_ref[...] = dg
    du_ref[...] = du
    dn_ref[...] = (dotd(dg, w_ref[:, 0:FFB], NT) + dotd(du, w_ref[:, FFB : 2 * FFB], NT)).astype(BF)
    out_ref[...] = dotd(act, w_ref[:, 2 * FFB : 3 * FFB], NT).astype(BF)


def wgrad_kernel(
    n0, n1, m0, m1, a0, a1, g0, g1, u0, u1, da_ref, att_ref, out_ref
):
    out_ref[:, 0:FFB] = (dotd(n0[...], g0[...], TN) + dotd(n1[...], g1[...], TN)).astype(BF)
    out_ref[:, FFB : 2 * FFB] = (dotd(n0[...], u0[...], TN) + dotd(n1[...], u1[...], TN)).astype(BF)
    out_ref[:, 2 * FFB : 3 * FFB] = (
        dotd(m0[...], a0[...], TN) + dotd(m1[...], a1[...], TN)
    ).astype(BF)
    out_ref[:, 3 * FFB :] = dotd(da_ref[...], att_ref[...], TN).astype(BF)


def call(kernel, outs, *args, name=None):
    return pl.pallas_call(
        kernel,
        out_shape=[jax.ShapeDtypeStruct(s, t) for s, t in outs],
        in_specs=[VMEM_ALL] * len(args),
        out_specs=[VMEM_ALL] * len(outs),
        compiler_params=PARAMS,
        name=name,
    )(*args)


def attn_fwd(bo, own, q, kv):
    return pl.pallas_call(
        attn_fwd_kernel,
        out_shape=[
            jax.ShapeDtypeStruct((2, 128, 512), BF),
            jax.ShapeDtypeStruct((2, 2, 448, 128), F32),
        ],
        grid_spec=pltpu.PrefetchScalarGridSpec(
            num_scalar_prefetch=2,
            grid=(2,),
            in_specs=[
                pl.BlockSpec((1, 2, 448, 128), lambda s, *_: (s, 0, 0, 0)),
                pl.BlockSpec((16, 1, 128, 128), lambda s, *_: (0, s, 0, 0)),
            ],
            out_specs=[
                pl.BlockSpec((1, 128, 512), lambda s, *_: (s, 0, 0)),
                pl.BlockSpec((1, 2, 448, 128), lambda s, *_: (s, 0, 0, 0)),
            ],
            scratch_shapes=[
                pltpu.VMEM((2048, 128), BF),
                pltpu.VMEM((8, 448, CH), F32),
                pltpu.VMEM((448, 128), F32),
                pltpu.VMEM((448, 128), F32),
                pltpu.VMEM((448, 128), F32),
            ],
        ),
        compiler_params=PARAMS,
        name="attn_fwd",
    )(bo, own, q, kv)


def attn_bwd(bo, own, q, kv, att, datt, lse):
    per_seq = pl.BlockSpec((1, 2, 448, 128), lambda s, *_: (s, 0, 0, 0))
    tokens = pl.BlockSpec((1, 128, 512), lambda s, *_: (s, 0, 0))
    pairs = pl.BlockSpec((16, 1, 128, 128), lambda s, *_: (0, s, 0, 0))
    return pl.pallas_call(
        attn_bwd_kernel,
        out_shape=[
            jax.ShapeDtypeStruct((2, 2, 448, 128), F32),
            jax.ShapeDtypeStruct((16, 2, 128, 128), BF),
        ],
        grid_spec=pltpu.PrefetchScalarGridSpec(
            num_scalar_prefetch=2,
            grid=(2,),
            in_specs=[per_seq, pairs, tokens, tokens, per_seq],
            out_specs=[per_seq, pairs],
            scratch_shapes=[
                pltpu.VMEM((2048, 128), BF),
                pltpu.VMEM((2048, 128), F32),
                pltpu.VMEM((448, 128), F32),
            ],
        ),
        compiler_params=PARAMS,
        name="attn_bwd",
    )(bo, own, q, kv, att, datt, lse)


def mlp(n, dm, w2):
    tok = pl.BlockSpec((256, DP), lambda i: (i, 0))
    hid = pl.BlockSpec((256, FFB), lambda i: (i, 0))
    return pl.pallas_call(
        mlp_kernel,
        out_shape=[jax.ShapeDtypeStruct((512, FFB), BF)] * 3
        + [jax.ShapeDtypeStruct((512, DP), BF)] * 2,
        grid=(2,),
        in_specs=[
            tok,
            tok,
            pl.BlockSpec((DP, 3 * FFB), lambda i: (0, 0), pipeline_mode=pl.Buffered(1)),
        ],
        out_specs=[hid, hid, hid, tok, tok],
        compiler_params=PARAMS,
        name="mlp",
    )(n, dm, w2)


def wgrads(n0, n1, m0, m1, first, second, da, att):
    feat = pl.BlockSpec((512, 256), lambda i: (0, i))
    hid = pl.BlockSpec((512, FFB), lambda i: (0, 0))
    args = [n0, n1, m0, m1, first[0], second[0], first[1], second[1], first[2], second[2], da, att]
    return pl.pallas_call(
        wgrad_kernel,
        out_shape=jax.ShapeDtypeStruct((DP, 3 * FFB + 512), BF),
        grid=(4,),
        in_specs=[feat] * 4
        + [hid] * 6
        + [
            pl.BlockSpec((256, 256), lambda i: (0, i)),
            pl.BlockSpec((256, 512), lambda i: (0, 0)),
        ],
        out_specs=pl.BlockSpec((256, 3 * FFB + 512), lambda i: (i, 0)),
        compiler_params=PARAMS,
        name="wgrad",
    )(*args)


def rms(v):
    scale = lax.rsqrt(jnp.sum(v * v, axis=-1, keepdims=True) * (1.0 / DM) + EPS)
    return v * scale, scale


def rms_back(dn, unit, scale, gain):
    e = dn * gain
    mean = jnp.sum(e * unit, axis=-1, keepdims=True) * (1.0 / DM)
    return scale * (e - unit * mean), jnp.sum(dn * unit, axis=0)


def pick(v, index):
    return lax.dynamic_index_in_dim(v, index, 0, keepdims=False)


def both(own, other, t):
    return jnp.stack([jnp.where(t == 0, own, other), jnp.where(t == 0, other, own)])


def scatter_fsdp(own, other):
    pair = own.astype(F32) + swap_tp(other).astype(F32)
    got = lax.all_to_all(
        pair.astype(BF).reshape(4, 128, DP), "fsdp", split_axis=0, concat_axis=0, tiled=True
    )
    return jnp.sum(got.astype(F32), axis=0)


def body(inputs, block_order, cotangent, gains, w_qkv, b_qkv, w_out, w_gate_up, w_down):
    seqs, toks, width = inputs.shape
    ctx = lax.axis_index("ctx")
    t = lax.axis_index("tp")
    owner = lax.axis_index("fsdp") * 16 + ctx
    sel = selection()

    bias_row = jnp.where(jnp.arange(HD) == owner, b_qkv[0, 0], jnp.zeros((), BF)).reshape(1, 9 * HD)
    patch1 = jnp.concatenate(
        [
            jnp.concatenate([w_qkv[0, :, 0, :], bias_row, jnp.zeros((1, 9 * HD), BF)], axis=0),
            jnp.pad(gains[0].T, ((0, 2), (0, HD - 2))),
        ],
        axis=1,
    )
    w1 = spread(patch1, OWNERS, GRP).reshape(DP, 640)

    tall = jnp.pad(w_gate_up[0], ((0, 2), (0, 0), (0, 4 * FFB - 2432)))
    gate_parts = tall[:, 0].reshape(SLOT, 4, FFB).transpose(1, 0, 2)
    up_parts = tall[:, 1].reshape(SLOT, 4, FFB).transpose(1, 0, 2)
    down_parts = (
        jnp.pad(w_down[0].T, ((0, 2), (0, 4 * FFB - 2432)))
        .reshape(SLOT, 4, FFB)
        .transpose(1, 0, 2)
    )
    out_part = jnp.broadcast_to(jnp.pad(w_out[0, 0].T, ((0, 2), (0, 64)))[None], (4, SLOT, 512))
    patch2 = jnp.concatenate([gate_parts, up_parts, down_parts, out_part], axis=2)
    send2 = jnp.broadcast_to(patch2[:, None], (4, 16, SLOT, 3 * FFB + 512)).reshape(
        OWNERS, SLOT, 3 * FFB + 512
    )
    w2 = lax.all_to_all(send2, GRP, split_axis=0, concat_axis=0, tiled=True).reshape(
        DP, 3 * FFB + 512
    )
    wo = w2[:, 3 * FFB :]

    own = lax.dynamic_slice_in_dim(block_order, 2 * ctx, 2, 1)
    pos = (own[:, :, None] * 64 + jnp.arange(64, dtype=jnp.int32)).reshape(seqs * toks, 1)
    lane = lax.broadcasted_iota(jnp.int32, (1, 128), 1)
    freq = jnp.exp((lane % 32).astype(F32) * (-2.0 * math.log(ROPE_BASE) / HD))
    angle = pos.astype(F32) * freq
    cosine = jnp.cos(angle)
    sine = jnp.where(lane % HD < HD // 2, -1.0, 1.0) * jnp.sin(angle)

    x = pad_features(inputs.reshape(seqs * toks, width), sel)
    g = pad_features(cotangent.reshape(seqs * toks, width), sel)
    xh = pick(x.reshape(2, 128, DP), t)
    gh = pick(g.reshape(2, 128, DP), t)
    m0 = spread(gh.astype(BF), 4, "fsdp").reshape(512, DP)
    m1 = swap_tp(m0)

    q, pairs, normed1, gain_rows = call(
        qkv_kernel,
        [((2, 2, 448, 128), BF), ((16, 256, 128), BF), ((256, DP), BF), ((8, DP), F32)],
        x, w1, cosine, sine, name="qkv",
    )
    gain1 = gain_rows[0:1]
    gain2 = gain_rows[1:2]
    kv = lax.all_to_all(pairs, "ctx", split_axis=0, concat_axis=0, tiled=True).reshape(
        16, 2, 128, 128
    )
    att, lse = attn_fwd(block_order, own, q, kv)
    att2 = att.reshape(256, 512)
    mixed = dotd(att2, wo, NT).reshape(2, 128, DP)
    h2 = xh + (pick(mixed, t) + swap_tp(pick(mixed, 1 - t).astype(BF)).astype(F32))
    unit2, scale2 = rms(h2)
    n0 = spread((unit2 * gain2).astype(BF), 4, "fsdp").reshape(512, DP)
    n1 = swap_tp(n0)
    first = mlp(n0, m0, w2)
    second = mlp(n1, m1, w2)

    dn2 = scatter_fsdp(first[3], second[3])
    back2, gg2 = rms_back(dn2, unit2, scale2, gain2)
    g2 = gh + back2
    dah = g2.astype(BF)
    da = both(dah, swap_tp(dah), t).reshape(256, DP)
    datt = dot(da, wo).astype(BF).reshape(2, 128, 512)
    big = wgrads(n0, n1, m0, m1, first, second, da, att2).reshape(OWNERS, SLOT, 3 * FFB + 512)
    big = lax.all_to_all(big, GRP, split_axis=0, concat_axis=0, tiled=True)

    dq, dkv = attn_bwd(block_order, own, q, kv, att, datt, lse)
    dkv = lax.all_to_all(dkv, "ctx", split_axis=0, concat_axis=0, tiled=True).reshape(16, 256, 128)
    dproj, dn1 = call(
        dproj_kernel, [((256, 640), BF), ((256, DP), F32)], dq, dkv, cosine, sine, w1, name="dproj"
    )
    dn1 = dn1.reshape(2, 128, DP)
    dn1h = pick(dn1, t) + swap_tp(pick(dn1, 1 - t).astype(BF)).astype(F32)
    unit1, scale1 = rms(xh)
    back1, gg1 = rms_back(dn1h, unit1, scale1, gain1)
    gin = unpad_features(g2 + back1, sel)
    grad_inputs = both(gin, swap_tp(gin), t)

    place = (jnp.arange(640)[None, :] == 576 + jnp.arange(2)[:, None]).astype(BF)
    gq = dotd(normed1, dproj, TN) + dotd(jnp.stack([gg1, gg2]).astype(BF), place, TN)
    gq = lax.all_to_all(
        gq.astype(BF).reshape(OWNERS, SLOT, 640), GRP, split_axis=0, concat_axis=0, tiled=True
    )

    outh = h2 + scatter_fsdp(first[4], second[4])
    outh = unpad_features(outh, sel)
    outputs = both(outh, swap_tp(outh), t)

    big = jnp.sum(big.reshape(4, 16, SLOT, 3 * FFB + 512).astype(F32), axis=1)
    hidden = big[:, :ROWS, : 3 * FFB].transpose(1, 0, 2)

    def columns(k):
        return hidden[:, :, k * FFB : k * FFB + FFB].reshape(ROWS, 4 * FFB)[:, :2432]

    grad_gate_up = jnp.stack([columns(0), columns(1)], axis=1)[None]
    grad_down = columns(2).T[None]
    grad_out = jnp.sum(big[:, :ROWS, 3 * FFB : 3 * FFB + 448], axis=0).T[None, None]
    gq = jnp.sum(gq.astype(F32), axis=0)
    grad_qkv = gq[None, :ROWS, None, :576]
    grad_bias = lax.dynamic_slice_in_dim(gq[ROWS, :576].reshape(9, HD), owner, 1, 1)[None, None]
    gg = gq[:ROWS, 576:578].T
    grad_gains = (gg + swap_tp(gg))[None]
    return (outputs, grad_inputs, grad_gains, grad_qkv, grad_bias, grad_out, grad_gate_up, grad_down)


def solution(mesh):
    in_specs = (
        P("fsdp", "ctx", None),
        P("fsdp", None),
        P("fsdp", "ctx", None),
        P(None, None, ("fsdp", "ctx")),
        P(None, ("fsdp", "ctx"), "tp", None),
        P(None, "tp", None, ("fsdp", "ctx")),
        P(None, "tp", None, ("fsdp", "ctx")),
        P(None, ("fsdp", "ctx"), None, "tp"),
        P(None, "tp", ("fsdp", "ctx")),
    )
    out_specs = (
        P("fsdp", "ctx", None),
        P("fsdp", "ctx", None),
        P(None, None, ("fsdp", "ctx")),
        P(None, ("fsdp", "ctx"), "tp", None),
        P(None, "tp", None, ("fsdp", "ctx")),
        P(None, "tp", None, ("fsdp", "ctx")),
        P(None, ("fsdp", "ctx"), None, "tp"),
        P(None, "tp", ("fsdp", "ctx")),
    )
    return jax.shard_map(body, mesh=mesh, in_specs=in_specs, out_specs=out_specs, check_vma=False)
```

time: 1460 us -> 398 us (0.27)
  blocking collectives: 705 us -> 23.2 us
  local copies, waits for them, and re-layouts: 171 us -> 21.7 us
  other arithmetic: 143 us -> 24.3 us
  waiting for transfers between devices: 279 us -> 183 us
  Pallas kernels: 0 us -> 63.6 us
  matrix products: 76.8 us -> 13.6 us
  between operations: 16.3 us -> 1.39 us
    all_gather x4 -> x0, blocking collectives: 705 us -> none  [the longest x1 192 us: body(): lax.all_gather(w_qkv[layer_index], ('fsdp', 'ctx'), axis=0, tiled=True)]
    all_to_all x6 -> x9, waiting for transfers between devices: 15.2 us -> 177 us  [the longest x1 49.9 us: body(): big = lax.all_to_all(big, GRP, split_axis=0, concat_axis=0, tiled=True)]
    all_gather x3 -> x0, waiting for transfers between devices: 121 us -> none  [the longest x1 64.1 us: body(): lax.all_gather(w_gate_up[layer_index], ('fsdp', 'ctx'), axis=0, tiled=True)]
    psum x3 -> x0, waiting for transfers between devices: 98.5 us -> none  [the longest x2 73 us: head_total(): return lax.psum(partial_rows, 'tp')]
    convert_element_type x15 -> x3, local copies, waits for them, and re-layouts: 70.3 us -> 1.27 us  [the longest x1 1.15 us: body(): dn1h = pick(dn1, t) + swap_tp(pick(dn1, 1 - t).astype(BF)).astype(F32)]
    pallas_call x0 -> x7, Pallas kernels: none -> 63.6 us  [the longest x2 17.6 us: mlp(): pl.pallas_call(mlp_kernel, out_shape=[jax.ShapeDtypeStruct((512, FFB), BF...]
    dot_general x18 -> x8, matrix products: 76.8 us -> 13.6 us  [the longest x5 6.96 us: dotd(): return lax.dot_general(a, b, dims, preferred_element_type=F32)]
    unnamed x101 -> x68, local copies, waits for them, and re-layouts: 66.2 us -> 9.9 us
  transfers between devices with their start and end apart: 13 -> 19, of which waited for: 8 -> 12; matrix products, arithmetic and copies ran while one was open for 20% -> 7% of each run, Pallas kernels for 0% -> 8%
where the time goes in v1:
time: 398 us; the launch traced here: 394 us
  waiting for transfers between devices  183 us (46%)
  Pallas kernels  63.6 us (16%)
  starting transfers between devices  63 us (16%)
  other arithmetic  24.3 us (6%)
  blocking collectives  23.2 us (6%)
  local copies, waits for them, and re-layouts  21.7 us (5%)
  matrix products  13.6 us (3%)
    all_to_all x1, waiting for transfers between devices, body(): big = lax.all_to_all(big, GRP, split_axis=0, concat_axis=0, tiled=True)  49.9 us
    all_to_all x1, waiting for transfers between devices, body(): lax.all_to_all(send2, GRP, split_axis=0, concat_axis=0, tiled=True)  42.3 us
    all_to_all x3, waiting for transfers between devices, spread(): return lax.all_to_all(full, axes, split_axis=0, concat_axis=0, tiled=True)  40.1 us
    all_to_all x2, waiting for transfers between devices, scatter_fsdp(): lax.all_to_all(pair.astype(BF).reshape(4, 128, DP), 'fsdp', split_axis=0,...  26.1 us
    all_to_all x1, blocking collectives, body(): lax.all_to_all(dkv, 'ctx', split_axis=0, concat_axis=0, tiled=True)  23.2 us
    all_to_all x3, starting transfers between devices, spread(): return lax.all_to_all(full, axes, split_axis=0, concat_axis=0, tiled=True)  17.8 us
    pallas_call x2, Pallas kernels, mlp(): pl.pallas_call(mlp_kernel, out_shape=[jax.ShapeDtypeStruct((512, FFB), BF...  17.6 us
    pallas_call x1, Pallas kernels, attn_bwd(): pl.pallas_call(attn_bwd_kernel, out_shape=[jax.ShapeDtypeStruct((2, 2, 44...  15.7 us
  transfers between devices with their start and end apart: 19, of which 12 were waited for; matrix products, arithmetic and copies ran while one was open for 7% of the time, Pallas kernels for 8%

profile of v1, /device:TPU:68, one launch (start us, length us, event | category | flops | bytes accessed | tf_op | source)
XLA Modules:
  0.0 393.8 jit_solution(14858906310041797559)
XLA Ops:
  4.3 10.6 %all-to-all-start = ((bf16[64,16,640]{2,1,0:T(8,128)(2,1)}), bf16[64,16,640]{2,1,0:T(8,128)(2,1)S(1)}, u32[]{:S(2)}, u32[]{:S(2)}) async-start(bf16[64,16,640]{2,1,0:T(8,128)(2,1)} %broadcast_in_dim.92), calls=%async_computation | async-start | bytes 2621440 | tf_op jit(solution)/shard_map/all_to_all | solution.py:71
  20.5 11.9 %all-to-all-done = bf16[64,16,640]{2,1,0:T(8,128)(2,1)S(1)} async-done(((bf16[64,16,640]{2,1,0:T(8,128)(2,1)}), bf16[64,16,640]{2,1,0:T(8,128)(2,1)S(1)}, u32[]{:S(2)}, u32[]{:S(2)}) %all-to-all-start) | async-done | bytes 1310752 | tf_op jit(solution)/shard_map/all_to_all | solution.py:71
  33.6 3.9 %qkv.1 = (bf16[2,2,448,128]{3,2,1,0:T(8,128)(2,1)}, bf16[16,256,128]{2,1,0:T(8,128)(2,1)}, bf16[256,1024]{1,0:T(8,128)(2,1)}, f32[8,1024]{1,0:T(8,128)}) custom-call(f32[256,1024]{1,0:T(8,128)} %slice_add_fusion.2.x_ref, bf16[1024,640]{1,0:T(8,128)(2,1)} %bitcast.143, f32[256,128]{1,0:T(8,128)} %get-tuple-element.97.cos_ref, ...), custom_call_target="tpu_custom_call" | custom-call | tf_op jit(solution)/shard_map/qkv/pallas_call | solution.py:270
  37.5 8.1 %all-to-all-start.1 = ((bf16[16,256,128]{2,1,0:T(8,128)(2,1)}), bf16[16,256,128]{2,1,0:T(8,128)(2,1)S(1)}, u32[]{:S(2)}, u32[]{:S(2)}) async-start(bf16[16,256,128]{2,1,0:T(8,128)(2,1)} %get-tuple-element.29), calls=%async_computation.1 | async-start | bytes 2097152 | tf_op jit(solution)/shard_map/all_to_all | solution.py:460
  46.8 10.8 %all-to-all-done.1 = bf16[16,256,128]{2,1,0:T(8,128)(2,1)S(1)} async-done(((bf16[16,256,128]{2,1,0:T(8,128)(2,1)}), bf16[16,256,128]{2,1,0:T(8,128)(2,1)S(1)}, u32[]{:S(2)}, u32[]{:S(2)}) %all-to-all-start.1) | async-done | bytes 1048608 | tf_op jit(solution)/shard_map/all_to_all | solution.py:460
  57.6 2.6 broadcast_in_dim.96
  60.2 9.5 %all-to-all-start.2 = ((bf16[64,16,2432]{2,1,0:T(8,128)(2,1)}), bf16[64,16,2432]{2,1,0:T(8,128)(2,1)}, u32[]{:S(2)}, u32[]{:S(2)}) async-start(bf16[64,16,2432]{2,1,0:T(8,128)(2,1)} %bitcast.138), calls=%async_computation.2 | async-start | bytes 9961472 | tf_op jit(solution)/shard_map/all_to_all | solution.py:433
  72.3 12.3 %attn_fwd.1 = (bf16[2,128,512]{2,1,0:T(8,128)(2,1)}, f32[2,2,448,128]{3,2,1,0:T(8,128)}) custom-call(s32[2,32]{1,0:T(2,128)} %bo_ref.3, s32[2,2]{1,0:T(2,128)} %get-tuple-element.69.own_ref, bf16[2,2,448,128]{3,2,1,0:T(8,128)(2,1)} %get-tuple-element.28.q_ref, bf16[16,2,128,128]{3,2,1,0:T(8,128)(2,1)} %bitcast.145), custom_call_target="tpu_custom_call" | custom-call | tf_op jit(solution)/shard_map/attn_fwd/pallas_call | solution.py:281
  84.6 42.3 %all-to-all-done.2 = bf16[64,16,2432]{2,1,0:T(8,128)(2,1)} async-done(((bf16[64,16,2432]{2,1,0:T(8,128)(2,1)}), bf16[64,16,2432]{2,1,0:T(8,128)(2,1)}, u32[]{:S(2)}, u32[]{:S(2)}) %all-to-all-start.2) | async-done | bytes 4980768 | tf_op jit(solution)/shard_map/all_to_all | solution.py:433
  130.0 3.7 all-to-all-start.4
  136.6 13.1 %all-to-all-done.4 = bf16[4,128,1024]{2,1,0:T(8,128)(2,1)S(1)} async-done(((bf16[4,128,1024]{2,1,0:T(8,128)(2,1)}), bf16[4,128,1024]{2,1,0:T(8,128)(2,1)S(1)}, u32[]{:S(2)}, u32[]{:S(2)}) %all-to-all-start.4) | async-done | bytes 1048608 | tf_op jit(solution)/shard_map/all_to_all | solution.py:71
  150.9 3.5 all-to-all-start.3
  154.6 15.1 %all-to-all-done.3 = bf16[4,128,1024]{2,1,0:T(8,128)(2,1)S(1)} async-done(((bf16[4,128,1024]{2,1,0:T(8,128)(2,1)}), bf16[4,128,1024]{2,1,0:T(8,128)(2,1)S(1)}, u32[]{:S(2)}, u32[]{:S(2)}) %all-to-all-start.3) | async-done | bytes 1048608 | tf_op jit(solution)/shard_map/all_to_all | solution.py:71
  169.7 2.7 collective-permute-done.1.n_ref.n1
  173.3 8.8 %mlp.3 = (bf16[512,640]{1,0:T(8,128)(2,1)}, bf16[512,640]{1,0:T(8,128)(2,1)}, bf16[512,640]{1,0:T(8,128)(2,1)}, bf16[512,1024]{1,0:T(8,128)(2,1)}, bf16[512,1024]{1,0:T(8,128)(2,1)}) custom-call(bf16[512,1024]{1,0:T(8,128)(2,1)} %copy-done.11, bf16[512,1024]{1,0:T(8,128)(2,1)} %collective-permute-done.2.dm_ref.m1, bf16[1024,2432]{1,0:T(8,128)(2,1)} %bitcast.18.w_ref), custom_call_target="tpu_custom_call" | custom-call | tf_op jit(solution)/shard_map/mlp/pallas_call | solution.py:340
  182.7 8.8 %mlp.2 = (bf16[512,640]{1,0:T(8,128)(2,1)}, bf16[512,640]{1,0:T(8,128)(2,1)}, bf16[512,640]{1,0:T(8,128)(2,1)}, bf16[512,1024]{1,0:T(8,128)(2,1)}, bf16[512,1024]{1,0:T(8,128)(2,1)}) custom-call(bf16[512,1024]{1,0:T(8,128)(2,1)} %bitcast.151, bf16[512,1024]{1,0:T(8,128)(2,1)} %bitcast.148, bf16[1024,2432]{1,0:T(8,128)(2,1)} %bitcast.18.w_ref), custom_call_target="tpu_custom_call" | custom-call | tf_op jit(solution)/shard_map/mlp/pallas_call | solution.py:340
  191.6 2.6 add_convert_fusion.1
  194.2 3.5 all-to-all-start.6
  198.7 3.0 add_convert_fusion.2
  201.7 11.7 %all-to-all-done.6 = bf16[4,128,1024]{2,1,0:T(8,128)(2,1)S(1)} async-done(((bf16[4,128,1024]{2,1,0:T(8,128)(2,1)}), bf16[4,128,1024]{2,1,0:T(8,128)(2,1)S(1)}, u32[]{:S(2)}, u32[]{:S(2)}) %all-to-all-start.6) | async-done | bytes 1048608 | tf_op jit(solution)/shard_map/all_to_all | solution.py:397
  213.3 4.2 %all-to-all-start.5 = ((bf16[4,128,1024]{2,1,0:T(8,128)(2,1)}), bf16[4,128,1024]{2,1,0:T(8,128)(2,1)}, u32[]{:S(2)}, u32[]{:S(2)}) async-start(bf16[4,128,1024]{2,1,0:T(8,128)(2,1)} %bitcast.28), calls=%async_computation.5 | async-start | bytes 2097152 | tf_op jit(solution)/shard_map/all_to_all | solution.py:397
  218.1 14.4 %all-to-all-done.5 = bf16[4,128,1024]{2,1,0:T(8,128)(2,1)} async-done(((bf16[4,128,1024]{2,1,0:T(8,128)(2,1)}), bf16[4,128,1024]{2,1,0:T(8,128)(2,1)}, u32[]{:S(2)}, u32[]{:S(2)}) %all-to-all-start.5) | async-done | bytes 1048608 | tf_op jit(solution)/shard_map/all_to_all | solution.py:397
  237.0 2.5 convolution_convert_fusion
  239.6 15.7 %attn_bwd.1 = (f32[2,2,448,128]{3,2,1,0:T(8,128)}, bf16[16,2,128,128]{3,2,1,0:T(8,128)(2,1)}) custom-call(s32[2,32]{1,0:T(2,128)} %bo_ref.3, s32[2,2]{1,0:T(2,128)} %get-tuple-element.69.own_ref, bf16[2,2,448,128]{3,2,1,0:T(8,128)(2,1)} %get-tuple-element.28.q_ref, bf16[16,2,128,128]{3,2,1,0:T(8,128)(2,1)} %bitcast.146, ...), custom_call_target="tpu_custom_call" | custom-call | tf_op jit(solution)/shard_map/attn_bwd/pallas_call | solution.py:315
  255.3 23.2 %all_to_all.50 = bf16[16,2,128,128]{3,2,1,0:T(8,128)(2,1)} all-to-all(bf16[16,2,128,128]{3,2,1,0:T(8,128)(2,1)} %get-tuple-element.38), channel_id=1, replica_groups=mesh['fsdp'=4,'ctx'=16,'tp'=2] {'ctx'}, dimensions={0} | all-to-all | bytes 2097152 | tf_op jit(solution)/shard_map/all_to_all | solution.py:483
  278.5 3.9 %dproj.1 = (bf16[256,640]{1,0:T(8,128)(2,1)}, f32[256,1024]{1,0:T(8,128)}) custom-call(f32[2,2,448,128]{3,2,1,0:T(8,128)} %get-tuple-element.37.dq_ref, bf16[16,256,128]{2,1,0:T(8,128)(2,1)} %bitcast.153, f32[256,128]{1,0:T(8,128)} %get-tuple-element.97.cos_ref, f32[256,128]{1,0:T(8,128)} %get-tuple-element.96.sin_ref, bf16[1024,640]{1,0:T(8,128)(2,1)} %bitcast.144), custom_call_target="tpu_custom_call" | custom-call | tf_op jit(solution)/shard_map/dproj/pallas_call | solution.py:270
  289.0 8.4 %all-to-all-start.8 = ((bf16[64,16,640]{2,1,0:T(8,128)(2,1)}), bf16[64,16,640]{2,1,0:T(8,128)(2,1)S(1)}, u32[]{:S(2)}, u32[]{:S(2)}) async-start(bf16[64,16,640]{2,1,0:T(8,128)(2,1)} %bitcast.44), calls=%async_computation.8 | async-start | bytes 2621440 | tf_op jit(solution)/shard_map/all_to_all | solution.py:496
  297.4 10.1 %wgrad.1 = bf16[1024,2432]{1,0:T(8,128)(2,1)} custom-call(bf16[512,1024]{1,0:T(8,128)(2,1)} %bitcast.152, bf16[512,1024]{1,0:T(8,128)(2,1)} %copy-done.11, bf16[512,1024]{1,0:T(8,128)(2,1)} %bitcast.149, bf16[512,1024]{1,0:T(8,128)(2,1)} %collective-permute-done.2.dm_ref.m1, bf16[512,640]{1,0:T(8,128)(2,1)} %get-tuple-element.42.a0, ...), custom_call_target="tpu_custom_call" | custom-call | tf_op jit(solution)/shard_map/wgrad/pallas_call | solution.py:360
  307.5 8.1 %all-to-all-done.8 = bf16[64,16,640]{2,1,0:T(8,128)(2,1)S(1)} async-done(((bf16[64,16,640]{2,1,0:T(8,128)(2,1)}), bf16[64,16,640]{2,1,0:T(8,128)(2,1)S(1)}, u32[]{:S(2)}, u32[]{:S(2)}) %all-to-all-start.8) | async-done | bytes 1310752 | tf_op jit(solution)/shard_map/all_to_all | solution.py:496
  316.6 9.8 %all-to-all-start.9 = ((bf16[64,16,2432]{2,1,0:T(8,128)(2,1)}), bf16[64,16,2432]{2,1,0:T(8,128)(2,1)}, u32[]{:S(2)}, u32[]{:S(2)}) async-start(bf16[64,16,2432]{2,1,0:T(8,128)(2,1)} %bitcast.139), calls=%async_computation.9 | async-start | bytes 9961472 | tf_op jit(solution)/shard_map/all_to_all | solution.py:480
  338.0 49.9 %all-to-all-done.9 = bf16[64,16,2432]{2,1,0:T(8,128)(2,1)} async-done(((bf16[64,16,2432]{2,1,0:T(8,128)(2,1)}), bf16[64,16,2432]{2,1,0:T(8,128)(2,1)}, u32[]{:S(2)}, u32[]{:S(2)}) %all-to-all-start.9) | async-done | bytes 4980768 | tf_op jit(solution)/shard_map/all_to_all | solution.py:480
  387.8 3.1 convert_reduce_fusion
  (170 shorter events, 50.6 us)
Async XLA Ops:
  0.6 14.3 %copy-start.28 = (s32[2,32]{1,0:T(2,128)S(1)}, s32[2,32]{1,0:T(2,128)}, u32[]{:S(2)}) copy-start(s32[2,32]{1,0:T(2,128)} %bo_ref.3) | copy-start | bytes 772
  0.6 16.4 %copy-start.18 = (f32[2,128,896]{2,1,0:T(8,128)S(1)}, f32[2,128,896]{2,1,0:T(8,128)}, u32[]{:S(2)}) copy-start(f32[2,128,896]{2,1,0:T(8,128)} %param.9) | copy-start | bytes 2752516
  4.3 28.1 %all-to-all-start = ((bf16[64,16,640]{2,1,0:T(8,128)(2,1)}), bf16[64,16,640]{2,1,0:T(8,128)(2,1)S(1)}, u32[]{:S(2)}, u32[]{:S(2)}) async-start(bf16[64,16,640]{2,1,0:T(8,128)(2,1)} %broadcast_in_dim.92), calls=%async_computation | async-start | bytes 2621440 | tf_op jit(solution)/shard_map/all_to_all | solution.py:71
  20.5 25.1 %copy-start.27 = (bf16[1,1,448,14]{2,3,1,0:T(8,128)(2,1)S(1)}, bf16[1,1,448,14]{2,3,1,0:T(8,128)(2,1)}, u32[]{:S(2)}) copy-start(bf16[1,1,448,14]{2,3,1,0:T(8,128)(2,1)} %param.15) | copy-start | bytes 37636
  20.5 25.1 %copy-start.26 = (bf16[1,2432,14]{1,2,0:T(8,128)(2,1)S(1)}, bf16[1,2432,14]{1,2,0:T(8,128)(2,1)}, u32[]{:S(2)}) copy-start(bf16[1,2432,14]{1,2,0:T(8,128)(2,1)} %param.17) | copy-start | bytes 204292
  20.5 25.2 %copy-start.25 = (bf16[1,14,2,2432]{3,2,1,0:T(2,128)(2,1)S(1)}, bf16[1,14,2,2432]{3,2,1,0:T(2,128)(2,1)}, u32[]{:S(2)}) copy-start(bf16[1,14,2,2432]{3,2,1,0:T(2,128)(2,1)} %param.16) | copy-start | bytes 408580
  37.5 20.1 %all-to-all-start.1 = ((bf16[16,256,128]{2,1,0:T(8,128)(2,1)}), bf16[16,256,128]{2,1,0:T(8,128)(2,1)S(1)}, u32[]{:S(2)}, u32[]{:S(2)}) async-start(bf16[16,256,128]{2,1,0:T(8,128)(2,1)} %get-tuple-element.29), calls=%async_computation.1 | async-start | bytes 2097152 | tf_op jit(solution)/shard_map/all_to_all | solution.py:460
  60.2 66.7 %all-to-all-start.2 = ((bf16[64,16,2432]{2,1,0:T(8,128)(2,1)}), bf16[64,16,2432]{2,1,0:T(8,128)(2,1)}, u32[]{:S(2)}, u32[]{:S(2)}) async-start(bf16[64,16,2432]{2,1,0:T(8,128)(2,1)} %bitcast.138), calls=%async_computation.2 | async-start | bytes 9961472 | tf_op jit(solution)/shard_map/all_to_all | solution.py:433
  72.2 57.7 %copy-start.12 = (f32[256,1024]{1,0:T(8,128)}, f32[256,1024]{1,0:T(8,128)S(1)}, u32[]{:S(2)}) copy-start(f32[256,1024]{1,0:T(8,128)S(1)} %slice_add_fusion) | copy-start | bytes 3145732
  128.7 5.8 %collective-permute-start = (bf16[128,1024]{1,0:T(8,128)(2,1)S(1)}, bf16[128,1024]{1,0:T(8,128)(2,1)}, u32[]{:S(2)}, u32[]{:S(2)}) collective-permute-start(bf16[128,1024]{1,0:T(8,128)(2,1)S(1)} %fusion.35), channel_id=1, source_target_pairs={{0,1},{1,0},{2,3},{3,2},{4,5},{5,4},{6,7},{7,6},{8,9},{9,8},{10,11... | collective-permute-start | bytes 786440 | tf_op jit(solution)/shard_map/ppermute | solution.py:75
  130.0 19.7 %all-to-all-start.4 = ((bf16[4,128,1024]{2,1,0:T(8,128)(2,1)}), bf16[4,128,1024]{2,1,0:T(8,128)(2,1)S(1)}, u32[]{:S(2)}, u32[]{:S(2)}) async-start(bf16[4,128,1024]{2,1,0:T(8,128)(2,1)} %broadcast_in_dim.99), calls=%async_computation.4 | async-start | bytes 2097152 | tf_op jit(solution)/shard_map/all_to_all | solution.py:71
  149.7 32.5 %copy-start.3 = (bf16[4,128,1024]{2,1,0:T(8,128)(2,1)}, bf16[4,128,1024]{2,1,0:T(8,128)(2,1)S(1)}, u32[]{:S(2)}) copy-start(bf16[4,128,1024]{2,1,0:T(8,128)(2,1)S(1)} %all-to-all-done.4) | copy-start | bytes 3145732
  150.9 18.7 %all-to-all-start.3 = ((bf16[4,128,1024]{2,1,0:T(8,128)(2,1)}), bf16[4,128,1024]{2,1,0:T(8,128)(2,1)S(1)}, u32[]{:S(2)}, u32[]{:S(2)}) async-start(bf16[4,128,1024]{2,1,0:T(8,128)(2,1)} %broadcast_in_dim.97), calls=%async_computation.3 | async-start | bytes 2097152 | tf_op jit(solution)/shard_map/all_to_all | solution.py:71
  154.5 15.2 %collective-permute-start.2 = (bf16[512,1024]{1,0:T(8,128)(2,1)S(1)}, bf16[512,1024]{1,0:T(8,128)(2,1)}, u32[]{:S(2)}, u32[]{:S(2)}) collective-permute-start(bf16[512,1024]{1,0:T(8,128)(2,1)S(1)} %bitcast.147), channel_id=1, source_target_pairs={{0,1},{1,0},{2,3},{3,2},{4,5},{5,4},{6,7},{7,6},{8,9},{9,8},{10,11... | collective-permute-start | bytes 3145736 | tf_op jit(solution)/shard_map/ppermute | solution.py:75
  169.7 12.5 %copy-start.4 = (bf16[4,128,1024]{2,1,0:T(8,128)(2,1)}, bf16[4,128,1024]{2,1,0:T(8,128)(2,1)S(1)}, u32[]{:S(2)}) copy-start(bf16[4,128,1024]{2,1,0:T(8,128)(2,1)S(1)} %all-to-all-done.3) | copy-start | bytes 3145732
  169.7 2.7 collective-permute-start.1
  182.2 9.4 %collective-permute-start.5 = (bf16[512,1024]{1,0:T(8,128)(2,1)}, bf16[512,1024]{1,0:T(8,128)(2,1)S(1)}, u32[]{:S(2)}, u32[]{:S(2)}) collective-permute-start(bf16[512,1024]{1,0:T(8,128)(2,1)} %get-tuple-element.35), channel_id=1, source_target_pairs={{0,1},{1,0},{2,3},{3,2},{4,5},{5,4},{6,7},{7,6},{8,9},{9,8},{10,11... | collective-permute-start | bytes 3145736 | tf_op jit(solution)/shard_map/ppermute | solution.py:75
  182.4 15.3 %collective-permute-start.3 = (bf16[512,1024]{1,0:T(8,128)(2,1)}, bf16[512,1024]{1,0:T(8,128)(2,1)S(1)}, u32[]{:S(2)}, u32[]{:S(2)}) collective-permute-start(bf16[512,1024]{1,0:T(8,128)(2,1)} %get-tuple-element.33), channel_id=1, source_target_pairs={{0,1},{1,0},{2,3},{3,2},{4,5},{5,4},{6,7},{7,6},{8,9},{9,8},{10,11... | collective-permute-start | bytes 3145736 | tf_op jit(solution)/shard_map/ppermute | solution.py:75
  194.2 19.2 %all-to-all-start.6 = ((bf16[4,128,1024]{2,1,0:T(8,128)(2,1)}), bf16[4,128,1024]{2,1,0:T(8,128)(2,1)S(1)}, u32[]{:S(2)}, u32[]{:S(2)}) async-start(bf16[4,128,1024]{2,1,0:T(8,128)(2,1)} %bitcast.32), calls=%async_computation.6 | async-start | bytes 2097152 | tf_op jit(solution)/shard_map/all_to_all | solution.py:397
  198.7 19.1 %copy-start.6 = (f32[128,1024]{1,0:T(8,128)S(1)}, f32[128,1024]{1,0:T(8,128)}, u32[]{:S(2)}) copy-start(f32[128,1024]{1,0:T(8,128)} %copy-done.5) | copy-start | bytes 1572868
  213.3 19.2 %all-to-all-start.5 = ((bf16[4,128,1024]{2,1,0:T(8,128)(2,1)}), bf16[4,128,1024]{2,1,0:T(8,128)(2,1)}, u32[]{:S(2)}, u32[]{:S(2)}) async-start(bf16[4,128,1024]{2,1,0:T(8,128)(2,1)} %bitcast.28), calls=%async_computation.5 | async-start | bytes 2097152 | tf_op jit(solution)/shard_map/all_to_all | solution.py:397
  217.8 16.2 %copy-start.13 = (f32[256,1024]{1,0:T(8,128)S(1)}, f32[256,1024]{1,0:T(8,128)}, u32[]{:S(2)}) copy-start(f32[256,1024]{1,0:T(8,128)} %copy-done.12) | copy-start | bytes 3145732
  235.4 1.5 collective-permute-start.6
  237.0 41.5 %copy-start.15 = (bf16[2,128,1024]{2,1,0:T(8,128)(2,1)}, bf16[2,128,1024]{2,1,0:T(8,128)(2,1)S(1)}, u32[]{:S(2)}) copy-start(bf16[2,128,1024]{2,1,0:T(8,128)(2,1)S(1)} %pad_maximum_fusion.2) | copy-start | bytes 1572868
  283.6 1.8 collective-permute-start.7
  289.0 26.5 %all-to-all-start.8 = ((bf16[64,16,640]{2,1,0:T(8,128)(2,1)}), bf16[64,16,640]{2,1,0:T(8,128)(2,1)S(1)}, u32[]{:S(2)}, u32[]{:S(2)}) async-start(bf16[64,16,640]{2,1,0:T(8,128)(2,1)} %bitcast.44), calls=%async_computation.8 | async-start | bytes 2621440 | tf_op jit(solution)/shard_map/all_to_all | solution.py:496
  315.5 10.9 %copy-start.23 = (bf16[128,1024]{1,0:T(8,128)(2,1)S(1)}, bf16[128,1024]{1,0:T(8,128)(2,1)}, u32[]{:S(2)}) copy-start(bf16[128,1024]{1,0:T(8,128)(2,1)} %get-tuple-element.89) | copy-start | bytes 786436
  315.5 10.9 %copy-start.24 = (bf16[128,1024]{1,0:T(8,128)(2,1)S(1)}, bf16[128,1024]{1,0:T(8,128)(2,1)}, u32[]{:S(2)}) copy-start(bf16[128,1024]{1,0:T(8,128)(2,1)} %get-tuple-element.90) | copy-start | bytes 786436
  316.6 71.2 %all-to-all-start.9 = ((bf16[64,16,2432]{2,1,0:T(8,128)(2,1)}), bf16[64,16,2432]{2,1,0:T(8,128)(2,1)}, u32[]{:S(2)}, u32[]{:S(2)}) async-start(bf16[64,16,2432]{2,1,0:T(8,128)(2,1)} %bitcast.139), calls=%async_computation.9 | async-start | bytes 9961472 | tf_op jit(solution)/shard_map/all_to_all | solution.py:480
  328.0 3.7 collective-permute-start.4
  331.1 2.8 collective-permute-start.8
  335.8 1.5 collective-permute-start.9
  (16 other events, 51.8 us)
